TPU v7x, 128 devices: a whole 4x4x4 slice. The times are simulated.
128 devices in a mesh: pair: 8 (over y, z_lo), virt: 16 (over z_hi, x, core).
Axes of the slice: x: 4, y: 4, z: 4 (z_hi: 2, z_lo: 2; z = z_hi * 2 + z_lo), core: 2. Of those that a mesh axis runs over, the one named last changes fastest.
Arguments:
- amplitudes: float32 [4096, 16384], P('pair', 'virt'), may hold values from -6 to 6
- integrals: bfloat16 [16384, 16384], P('pair', 'virt'), may hold values from -0.046875 to 0.046875
- occ_energy: float32 [4096], P('pair'), may hold values from 0.5 to 4
- vir_energy: float32 [16384], P('virt'), may hold values from 0.5 to 4
- tile_mask: int32 [512, 128], P('pair', 'virt'), may hold values 0 or 1
- partner_slot: int32 [512, 128], P('pair', 'virt'), may hold values from 0 to 127, as said below
Outputs:
- new_amplitudes: float32 [4096, 16384], P('pair', 'virt')
Inputs may be any that keep to these rules, and one draw needn't show every extreme that they name: `partner_slot`: within the block of tiles of each device (tile rows of one pair index by tile columns of one virt index), every device number 0 to 127 stands exactly 4 times, in an order drawn from the seed.
All inputs are finite; a program needn't handle non-finite values. No bound on the sum of `tile_mask` on one device may be relied on, other than what follows from the above.
Results may differ from a plain program's by a relative error of at most 0.0012.
Values may be sent and summed in bfloat16 or wider, within the bound.
No kernel may reach another device: no remote copies, remote signals or barrier semaphores. Data moves between devices by JAX's collectives and lax.ppermute only.
A program may use at most 128 MiB of HBM per device.

v0:
```python
import jax
import jax.numpy as jnp
from jax import lax
from jax.sharding import PartitionSpec as P

TR = 8
TC = 128


def shards(amplitudes, integrals, occ_energy, vir_energy, tile_mask, partner_slot):
    row_count, col_count = amplitudes.shape
    amp_half = amplitudes.astype(jnp.bfloat16)
    pair_count = lax.axis_size("pair")
    virt_count = lax.axis_size("virt")
    full_panels = lax.all_gather(amp_half, "virt", axis=1, tiled=True)
    ladder = jnp.dot(
        full_panels,
        lax.all_gather(integrals, "pair", axis=0, tiled=True),
        preferred_element_type=jnp.float32,
    )
    row_tiles = row_count // TR
    col_tiles = col_count // TC
    tile_total = row_tiles * col_tiles
    weights = tile_mask.astype(jnp.float32)
    masked = ladder.reshape(row_tiles, TR, col_tiles, TC) * weights[:, None, :, None]
    tiles = masked.transpose(0, 2, 1, 3).reshape(tile_total, TR * TC)
    slots = partner_slot.reshape(tile_total)
    ordering = jnp.argsort(slots, stable=True)
    inverse = jnp.argsort(ordering, stable=True)
    device_count = pair_count * virt_count
    per_peer = tile_total // device_count
    outgoing = jnp.take(tiles, ordering, axis=0)
    incoming = lax.all_to_all(
        outgoing.reshape(device_count, per_peer, TR * TC),
        ("pair", "virt"),
        split_axis=0,
        concat_axis=0,
        tiled=True,
    )
    partner = jnp.take(incoming.reshape(tile_total, TR * TC), inverse, axis=0)
    symmetric = (
        (tiles + partner)
        .reshape(row_tiles, col_tiles, TR, TC)
        .transpose(0, 2, 1, 3)
        .reshape(row_count, col_count)
    )
    denominator = occ_energy[:, None] + vir_energy[None, :]
    return amplitudes - symmetric / denominator


def solution(mesh):
    in_specs = (
        P("pair", "virt"),
        P("pair", "virt"),
        P("pair"),
        P("virt"),
        P("pair", "virt"),
        P("pair", "virt"),
    )
    out_specs = P("pair", "virt")
    return jax.shard_map(shards, mesh=mesh, in_specs=in_specs, out_specs=out_specs, check_vma=False)
```

profile of v0, /device:TPU:1, one launch (start us, length us, event | category | flops | bytes accessed | tf_op | source)
XLA Modules:
  0.0 852.6 jit_solution(5119973933379959296)
XLA Ops:
  6.5 0.0 all-gather.3.cloned.1.call-start
  6.5 2.7 convert_element_type.6
  9.3 0.0 all-gather.3.cloned.1.call-update
  9.3 0.0 copy-start.4
  9.3 0.0 copy-start.3
  9.3 0.0 all-gather.5.cloned.1.call-start
  9.4 0.7 all-gather.5.cloned.1.call-update
  10.1 0.0 copy-done.4
  10.1 0.1 copy.8
  10.2 0.0 copy-done.3
  10.2 0.1 copy.9
  10.3 0.1 reshape.31
  10.4 3.8 sort.31
  14.2 109.1 %all-gather.3.cloned.1.call-done = bf16[512,16384]{1,0:T(8,128)(2,1)} async-done(((bf16[512,1024]{1,0:T(8,128)(2,1)}), bf16[512,16384]{1,0:T(8,128)(2,1)}) %all-gather.3.cloned.1.call-update) | async-done | bytes 16777232 | tf_op jit(solution)/shard_map/all_gather | solution.py:15
  123.3 638.9 %all-gather.5.cloned.1.call-done = bf16[16384,1024]{1,0:T(8,128)(2,1)} async-done(((bf16[2048,1024]{1,0:T(8,128)(2,1)}), bf16[16384,1024]{1,0:T(8,128)(2,1)}) %all-gather.5.cloned.1.call-update) | async-done | bytes 33554448 | tf_op jit(solution)/shard_map/all_gather | solution.py:18
  762.1 27.1 %fusion.1 = f32[64,8,8,128]{3,2,1,0:T(8,128)S(1)} fusion(bf16[512,16384]{1,0:T(8,128)(2,1)} %all-gather.3.cloned.1.call-done, bf16[16384,1024]{1,0:T(8,128)(2,1)} %all-gather.5.cloned.1.call-done, f32[64,8]{1,0:T(8,128)S(1)} %copy.8), kind=kOutput, calls=%fused_computation.6 | convolution fusion | flops 17180393472 | bytes 52430848 | tf_op jit(solution)/shard_map/dot_general | solution.py:16
  789.3 0.0 copy-start.1
  789.3 0.5 copy.16
  789.8 0.9 copy-done.1
  790.6 2.6 gather_fusion
  793.3 1.8 broadcast_select_fusion
  795.1 1.6 reshape.32
  796.7 9.9 %all-to-all-start = ((f32[128,4,1024]{2,1,0:T(4,128)}), f32[128,4,1024]{2,1,0:T(4,128)}, u32[]{:S(2)}, u32[]{:S(2)}) async-start(f32[128,4,1024]{2,1,0:T(4,128)} %reshape.32), calls=%async_computation | async-start | bytes 4194304 | tf_op jit(solution)/shard_map/all_to_all | solution.py:33
  806.6 3.8 sort.32
  810.4 26.0 %all-to-all-done = f32[128,4,1024]{2,1,0:T(4,128)} async-done(((f32[128,4,1024]{2,1,0:T(4,128)}), f32[128,4,1024]{2,1,0:T(4,128)}, u32[]{:S(2)}, u32[]{:S(2)}) %all-to-all-start) | async-done | bytes 2097184 | tf_op jit(solution)/shard_map/all_to_all | solution.py:33
  836.4 2.0 reshape.33
  838.4 2.7 gather_fusion.1
  841.0 0.0 copy-start
  841.0 0.0 copy-start.2
  841.0 0.0 copy-start.5
  841.0 2.9 fusion.2
  843.9 0.0 copy-done
  843.9 0.0 copy-done.2
  843.9 0.0 copy-done.5
  843.9 1.9 fusion
  (9 shorter events, 0.0 us)
Async XLA Ops:
  6.5 116.7 %all-gather.3.cloned.1.call-start = ((), (), s32[]{:S(2)}) async-start(), calls=%async_computation.1 | async-start | bytes 17825792 | tf_op jit(solution)/shard_map/all_gather | solution.py:15
  9.3 0.8 copy-start.4
  9.3 0.9 copy-start.3
  9.3 752.8 %all-gather.5.cloned.1.call-start = ((), (), s32[]{:S(2)}) async-start(), calls=%async_computation.2 | async-start | bytes 37748736 | tf_op jit(solution)/shard_map/all_gather | solution.py:18
  789.3 1.4 copy-start.1
  796.7 39.7 %all-to-all-start = ((f32[128,4,1024]{2,1,0:T(4,128)}), f32[128,4,1024]{2,1,0:T(4,128)}, u32[]{:S(2)}, u32[]{:S(2)}) async-start(f32[128,4,1024]{2,1,0:T(4,128)} %reshape.32), calls=%async_computation | async-start | bytes 4194304 | tf_op jit(solution)/shard_map/all_to_all | solution.py:33
  841.0 2.9 copy-start
  841.0 2.9 copy-start.2
  841.0 2.9 copy-start.5
Sparse Core Ops, SparseCore 0:
  9.8 113.4 all-gather.2
  124.9 637.1 all-gather.4
where the time goes:
time: 853 us
  waiting for transfers between devices  775 us (91%)
  matrix products  27.1 us (3%)
  other arithmetic  16.9 us (2%)
  between operations  13.5 us (2%)
  local copies, waits for them, and re-layouts  10.5 us (1%)
  starting transfers between devices  9.9 us (1%)
    all_gather x1, waiting for transfers between devices, shards(): lax.all_gather(integrals, 'pair', axis=0, tiled=True)  639 us
    all_gather x1, waiting for transfers between devices, shards(): full_panels = lax.all_gather(amp_half, 'virt', axis=1, tiled=True)  109 us
    dot_general x1, matrix products, shards(): jnp.dot(full_panels, lax.all_gather(integrals, 'pair', axis=0, tiled=True...  27.1 us
    all_to_all x1, waiting for transfers between devices, shards(): lax.all_to_all(outgoing.reshape(device_count, per_peer, TR * TC), ('pair'...  26 us
  transfers between devices with their start and end apart: 3, of which 3 were waited for; matrix products, arithmetic and copies ran while one was open for 1% of the time, Pallas kernels for 0%

commit v1 on v0

--- a/solution.py
+++ b/solution.py
@@ -12,7 +12,9 @@
     amp_half = amplitudes.astype(jnp.bfloat16)
     pair_count = lax.axis_size("pair")
     virt_count = lax.axis_size("virt")
-    full_panels = lax.all_gather(amp_half, "virt", axis=1, tiled=True)
+    full_panels = jnp.concatenate(
+        lax.all_to_all(jnp.stack([amp_half] * lax.axis_size("virt")), "virt", 0, 0), axis=1
+    )
     ladder = jnp.dot(
         full_panels,
         lax.all_gather(integrals, "pair", axis=0, tiled=True),

time: 853 us -> 967 us (1.13)
  local copies, waits for them, and re-layouts: 10.5 us -> 107 us
  waiting for transfers between devices: 775 us -> 786 us
    all_to_all x0 -> x1, waiting for transfers between devices: none -> 300 us  [shards(): lax.all_to_all(jnp.stack([amp_half] * lax.axis_size('virt')), 'virt', 0, 0)]
    all_gather x1, waiting for transfers between devices: 639 us -> 459 us  [shards(): lax.all_gather(integrals, 'pair', axis=0, tiled=True)]
    all_gather x1 -> x0, waiting for transfers between devices: 109 us -> none  [shards(): full_panels = lax.all_gather(amp_half, 'virt', axis=1, tiled=True)]
    dot_general x0 -> x2, local copies, waits for them, and re-layouts: none -> 69.7 us  [shards(): jnp.dot(full_panels, lax.all_gather(integrals, 'pair', axis=0, tiled=True...]
    reshape x0 -> x1, local copies, waits for them, and re-layouts: none -> 18.7 us  [shards(): jnp.concatenate(lax.all_to_all(jnp.stack([amp_half] * lax.axis_size('virt...]
  transfers between devices with their start and end apart: 3 -> 3, of which waited for: 3 -> 3; matrix products, arithmetic and copies ran while one was open for 1% -> 6% of each run, Pallas kernels for 0% -> 0%
where the time goes in v1:
time: 967 us; the launch traced here: 965 us
  waiting for transfers between devices  786 us (81%)
  local copies, waits for them, and re-layouts  107 us (11%)
  matrix products  24.8 us (3%)
  starting transfers between devices  19.1 us (2%)
  other arithmetic  15.4 us (2%)
  between operations  13.5 us (1%)
    all_gather x1, waiting for transfers between devices, shards(): lax.all_gather(integrals, 'pair', axis=0, tiled=True)  459 us
    all_to_all x1, waiting for transfers between devices, shards(): lax.all_to_all(jnp.stack([amp_half] * lax.axis_size('virt')), 'virt', 0, 0)  300 us
    dot_general x2, local copies, waits for them, and re-layouts, shards(): jnp.dot(full_panels, lax.all_gather(integrals, 'pair', axis=0, tiled=True...  69.7 us
    all_to_all x1, waiting for transfers between devices, shards(): lax.all_to_all(outgoing.reshape(device_count, per_peer, TR * TC), ('pair'...  26 us
    dot_general x1, matrix products, shards(): jnp.dot(full_panels, lax.all_gather(integrals, 'pair', axis=0, tiled=True...  24.8 us
  transfers between devices with their start and end apart: 3, of which 3 were waited for; matrix products, arithmetic and copies ran while one was open for 6% of the time, Pallas kernels for 0%

profile of v1, /device:TPU:1, one launch (start us, length us, event | category | flops | bytes accessed | tf_op | source)
XLA Modules:
  0.0 965.1 jit_solution(13276750915044412764)
XLA Ops:
  6.5 0.0 copy-start
  6.5 0.0 all-gather.2.cloned.1.call-start
  6.5 0.7 all-gather.2.cloned.1.call-update
  7.3 0.9 copy-done
  8.1 0.2 convert_element_type.6
  8.3 6.0 stack.2
  14.3 0.0 copy-start.7
  14.3 0.0 copy-start.6
  14.3 9.2 all-to-all-start
  23.5 0.0 copy-done.7
  23.5 0.1 copy.14
  23.6 0.0 copy-done.6
  23.6 0.1 copy.15
  23.7 0.1 reshape.38
  23.8 3.8 sort.31
  27.6 0.0 copy-start.2
  27.6 0.6 pad_clamp_fusion.1
  28.2 0.6 compare_and_fusion.1
  28.8 300.4 %all-to-all-done = bf16[16,512,1024]{2,1,0:T(8,128)(2,1)} async-done(((bf16[16,512,1024]{2,1,0:T(8,128)(2,1)}), bf16[16,512,1024]{2,1,0:T(8,128)(2,1)}, u32[]{:S(2)}, u32[]{:S(2)}) %all-to-all-start) | async-done | bytes 16777248 | tf_op jit(solution)/shard_map/all_to_all | solution.py:16
  329.2 18.7 %copy.12 = bf16[512,16,1024]{2,1,0:T(8,128)(2,1)} copy(bf16[512,16,1024]{2,0,1:T(8,128)(2,1)} %bitcast) | data formatting | bytes 33554432 | tf_op jit(solution)/shard_map/reshape | solution.py:15
  347.9 0.0 copy-done.2
  347.9 25.7 %reshape.65 = bf16[64,8,16384,1]{2,1,0,3:T(8,128)(2,1)} reshape(bf16[512,16,1024]{2,1,0:T(8,128)(2,1)} %copy.12) | data formatting | bytes 33554432 | tf_op jit(solution)/shard_map/dot_general | solution.py:18
  373.5 458.5 %all-gather.2.cloned.1.call-done = bf16[16384,1024]{1,0:T(8,128)(2,1)} async-done(((bf16[2048,1024]{1,0:T(8,128)(2,1)}), bf16[16384,1024]{1,0:T(8,128)(2,1)}) %all-gather.2.cloned.1.call-update) | async-done | bytes 33554448 | tf_op jit(solution)/shard_map/all_gather | solution.py:20
  832.1 44.0 %copy.13 = bf16[1024,16384]{1,0:T(8,128)(2,1)} copy(bf16[1024,16384]{0,1:T(8,128)(2,1)} %bitcast.31) | data formatting | bytes 67108864 | tf_op jit(solution)/shard_map/dot_general | solution.py:18
  876.1 24.8 %multiply_bitcast_fusion = f32[64,8,8,128]{3,2,1,0:T(8,128)} fusion(bf16[8,128,16384,1]{2,1,0,3:T(8,128)(2,1)} %bitcast.32, bf16[64,8,16384,1]{2,1,0,3:T(8,128)(2,1)} %reshape.65, f32[64,8]{1,0:T(8,128)S(1)} %copy.14), kind=kOutput, calls=%fused_computation.9 | convolution fusion | flops 17180393472 | bytes 52430848 | tf_op jit(solution)/shard_map/dot_general | solution.py:18
  900.9 0.0 copy-start.4
  900.9 2.1 copy.23
  903.0 0.0 copy-done.4
  903.0 0.0 copy-start.9
  903.0 2.7 gather_fusion
  905.7 0.0 copy-done.9
  905.7 1.8 broadcast_select_fusion
  907.5 1.6 reshape.39
  909.1 0.0 copy-start.3
  909.1 9.9 %all-to-all-start.1 = ((f32[128,4,1024]{2,1,0:T(4,128)}), f32[128,4,1024]{2,1,0:T(4,128)}, u32[]{:S(2)}, u32[]{:S(2)}) async-start(f32[128,4,1024]{2,1,0:T(4,128)} %reshape.39), calls=%async_computation.1 | async-start | bytes 4194304 | tf_op jit(solution)/shard_map/all_to_all | solution.py:35
  919.0 0.0 copy-done.3
  919.0 3.8 sort.32
  922.8 26.0 %all-to-all-done.1 = f32[128,4,1024]{2,1,0:T(4,128)} async-done(((f32[128,4,1024]{2,1,0:T(4,128)}), f32[128,4,1024]{2,1,0:T(4,128)}, u32[]{:S(2)}, u32[]{:S(2)}) %all-to-all-start.1) | async-done | bytes 2097184 | tf_op jit(solution)/shard_map/all_to_all | solution.py:35
  948.8 2.0 reshape.40
  950.8 2.7 gather_fusion.1
  953.5 0.0 copy-start.1
  953.5 0.0 copy-start.5
  953.5 0.0 copy-start.8
  953.5 2.9 fusion.3
  956.4 0.0 copy-done.1
  956.4 0.0 copy-done.5
  956.4 0.0 copy-done.8
  956.4 1.9 fusion.2
  (7 shorter events, 0.0 us)
Async XLA Ops:
  6.5 1.6 copy-start
  6.5 825.5 %all-gather.2.cloned.1.call-start = ((), (), s32[]{:S(2)}) async-start(), calls=%async_computation.2 | async-start | bytes 37748736 | tf_op jit(solution)/shard_map/all_gather | solution.py:20
  14.3 9.3 copy-start.7
  14.3 9.4 copy-start.6
  14.3 314.9 %all-to-all-start = ((bf16[16,512,1024]{2,1,0:T(8,128)(2,1)}), bf16[16,512,1024]{2,1,0:T(8,128)(2,1)}, u32[]{:S(2)}, u32[]{:S(2)}) async-start(bf16[16,512,1024]{2,1,0:T(8,128)(2,1)} %stack.2), calls=%async_computation | async-start | bytes 33554432 | tf_op jit(solution)/shard_map/all_to_all | solution.py:16
  27.6 320.3 %copy-start.2 = (s32[512]{0:T(512)}, s32[512]{0:T(512)S(1)}, u32[]{:S(2)}) copy-start(s32[512]{0:T(512)S(1)} %get-tuple-element.8) | copy-start | bytes 6148
  900.9 2.1 copy-start.4
  903.0 2.7 copy-start.9
  909.1 9.9 %copy-start.3 = (s32[512]{0:T(512)S(1)}, s32[512]{0:T(512)}, u32[]{:S(2)}) copy-start(s32[512]{0:T(512)} %copy-done.2) | copy-start | bytes 6148
  909.1 39.7 %all-to-all-start.1 = ((f32[128,4,1024]{2,1,0:T(4,128)}), f32[128,4,1024]{2,1,0:T(4,128)}, u32[]{:S(2)}, u32[]{:S(2)}) async-start(f32[128,4,1024]{2,1,0:T(4,128)} %reshape.39), calls=%async_computation.1 | async-start | bytes 4194304 | tf_op jit(solution)/shard_map/all_to_all | solution.py:35
  953.5 2.9 copy-start.1
  953.5 2.9 copy-start.5
  953.5 2.9 copy-start.8
Sparse Core Ops, SparseCore 0:
  9.0 823.0 all-gather.1
